TPU v7x, 32 devices: a whole 2x2x4 slice. The times are simulated.
32 devices in a mesh: row: 4 (over x, core), col: 8 (over z, y).
Axes of the slice: x: 2, y: 2, z: 4, core: 2. Of those that a mesh axis runs over, the one named last changes fastest.
Arguments:
- tokens: bfloat16 [128, 12288], P('col', 'row'), may hold values from -6 to 6
- w_in: bfloat16 [12288, 24576], P('row', 'col'), may hold values from -0.078125 to 0.078125
- w_out: bfloat16 [24576, 12288], P('col', 'row'), may hold values from -0.0546875 to 0.0546875
- mask_in: int32 [96, 192], P('row', 'col'), may hold values 0 or 1
- mask_out: int32 [192, 96], P('col', 'row'), may hold values 0 or 1
- out_grad: bfloat16 [128, 12288], P('col', 'row'), may hold values from -1.5 to 1.5
Outputs:
- mixed: bfloat16 [128, 12288], P('col', 'row')
- tokens_grad: bfloat16 [128, 12288], P('col', 'row')
- w_in_grad: bfloat16 [12288, 24576], P('row', 'col')
- w_out_grad: bfloat16 [24576, 12288], P('col', 'row')
Inputs may be any that keep to these rules, and one draw needn't show every extreme that they name: `mask_in`: one flag per block. `mask_out`: one flag per block.
All inputs are finite; a program needn't handle non-finite values.
Results may differ from a plain program's by a relative error of at most 0.0049.
Values may be sent and summed in bfloat16 or wider, within the bound.
A program may use at most 192 MiB of HBM per device.

v0:
```python
import jax
import jax.numpy as jnp
from jax import lax
from jax.sharding import PartitionSpec as P

BLK = 128


def apply_mask(weight, mask, blk):
    rows, cols = weight.shape
    shaped = weight.reshape(rows // blk, blk, cols // blk, blk)
    return (shaped * mask[:, None, :, None].astype(weight.dtype)).reshape(rows, cols)


def gelu_tanh(value):
    return jax.nn.gelu(value, approximate=True)


def contract(left, weight, dim):
    return lax.dot_general(
        left, weight, (((1,), (dim,)), ((), ())), preferred_element_type=jnp.float32
    )


def hidden_sum(left, weight, dim):
    return lax.psum_scatter(contract(left, weight, dim), "row", scatter_dimension=0, tiled=True)


def all_tokens(share):
    return lax.all_gather(share, "row", axis=0, tiled=True)


def column_sum(left, weight, dim):
    return lax.psum_scatter(contract(left, weight, dim), "col", scatter_dimension=0, tiled=True)


def local(tokens, w_in, w_out, mask_in, mask_out, out_grad):
    win = apply_mask(w_in, mask_in, BLK)
    wout = apply_mask(w_out, mask_out, BLK)
    gathered, grad_rows = (
        lax.all_gather(tokens, "col", axis=0, tiled=True),
        lax.all_gather(out_grad, "col", axis=0, tiled=True),
    )
    hidden = hidden_sum(gathered, win, 0)
    act_all = all_tokens(gelu_tanh(hidden).astype(jnp.bfloat16))
    mixed = column_sum(act_all, wout, 0).astype(jnp.bfloat16)
    act_grad = hidden_sum(grad_rows, wout, 1)
    unused, pull = jax.vjp(gelu_tanh, hidden)
    hid_all = all_tokens(pull(act_grad)[0].astype(jnp.bfloat16))
    outer_out = lax.dot_general(
        act_all, grad_rows, (((0,), (0,)), ((), ())), preferred_element_type=jnp.float32
    )
    w_out_grad = apply_mask(outer_out, mask_out, BLK).astype(jnp.bfloat16)
    tokens_grad = column_sum(hid_all, win, 1).astype(jnp.bfloat16)
    outer_in = lax.dot_general(
        gathered, hid_all, (((0,), (0,)), ((), ())), preferred_element_type=jnp.float32
    )
    w_in_grad = apply_mask(outer_in, mask_in, BLK).astype(jnp.bfloat16)
    return (mixed, tokens_grad, w_in_grad, w_out_grad)


def solution(mesh):
    return jax.shard_map(
        local,
        mesh=mesh,
        in_specs=(
            P("col", "row"),
            P("row", "col"),
            P("col", "row"),
            P("row", "col"),
            P("col", "row"),
            P("col", "row"),
        ),
        out_specs=(P("col", "row"), P("col", "row"), P("row", "col"), P("col", "row")),
        check_vma=False,
    )
```

profile of v0, /device:TPU:0, one launch (start us, length us, event | category | flops | bytes accessed | tf_op | source)
XLA Modules:
  0.0 315.8 jit_solution(14303630115790699037)
XLA Ops:
  7.2 0.0 reduce-scatter.15.cloned.1.call-start
  7.2 0.8 fusion.15
  8.0 34.1 %all_gather.14 = bf16[128,3072]{1,0:T(8,128)(2,1)S(1)} all-gather(bf16[16,3072]{1,0:T(8,128)(2,1)} %param.11), channel_id=1, replica_groups=mesh['row'=4,'col'=8] {'col'}, dimensions={0}, use_global_device_ids=true | all-gather | bytes 884736 | tf_op jit(solution)/shard_map/all_gather | solution.py:42
  42.1 6.8 %mul.98 = bf16[24,128,24,128]{3,2,1,0:T(8,128)(2,1)} broadcast(bf16[24,24]{1,0:T(8,128)(2,1)S(1)} %get-tuple-element.19), dimensions={0,2} | broadcast | bytes 18875520 | tf_op jit(solution)/shard_map/mul | solution.py:12
  48.9 14.4 %fusion.6 = f32[128,3072]{0,1:T(8,128)S(1)} fusion(bf16[128,3072]{1,0:T(8,128)(2,1)S(1)} %all_gather.14, bf16[3072,3072]{1,0:T(8,128)(2,1)} %param.8, bf16[384,8,24,128]{3,2,1,0:T(8,128)(2,1)} %bitcast.48), kind=kOutput, calls=%fused_computation.10 | convolution fusion | flops 2425356288 | bytes 40108032 | tf_op jit(solution)/shard_map/dot_general | solution.py:20
  63.3 1.6 copy.28
  65.0 0.0 reduce-scatter.15.cloned.1.call-update
  65.0 0.0 reduce-scatter.13.cloned.1.call-start
  65.1 32.1 %all_gather.12 = bf16[128,3072]{1,0:T(8,128)(2,1)S(1)} all-gather(bf16[16,3072]{1,0:T(8,128)(2,1)S(1)} %copy-done), channel_id=1, replica_groups=mesh['row'=4,'col'=8] {'col'}, dimensions={0}, use_global_device_ids=true | all-gather | bytes 884736 | tf_op jit(solution)/shard_map/all_gather | solution.py:41
  97.2 6.8 %mul.91 = bf16[24,128,24,128]{3,2,1,0:T(8,128)(2,1)} broadcast(bf16[24,24]{1,0:T(8,128)(2,1)S(1)} %get-tuple-element.21), dimensions={0,2} | broadcast | bytes 18875520 | tf_op jit(solution)/shard_map/mul | solution.py:12
  104.0 14.0 %fusion.7 = f32[128,3072]{0,1:T(8,128)S(1)} fusion(bf16[128,3072]{1,0:T(8,128)(2,1)S(1)} %all_gather.12, bf16[3072,3072]{1,0:T(8,128)(2,1)} %param.7, bf16[384,8,24,128]{3,2,1,0:T(8,128)(2,1)} %bitcast.50), kind=kOutput, calls=%fused_computation.11 | convolution fusion | flops 2425356288 | bytes 40108032 | tf_op jit(solution)/shard_map/dot_general | solution.py:20
  118.0 1.6 copy.26
  119.7 0.0 reduce-scatter.13.cloned.1.call-update
  119.7 0.0 reduce-scatter.11.cloned.1.call-start
  119.7 0.0 reduce-scatter.15.cloned.1.call-done
  119.8 29.0 %reduce-scatter.13.cloned.1.call-done = f32[32,3072]{1,0:T(8,128)} async-done(((f32[128,3072]{1,0:T(8,128)}), f32[32,3072]{1,0:T(8,128)}) %reduce-scatter.13.cloned.1.call-update) | async-done | bytes 393232 | tf_op jit(solution)/shard_map/reduce_scatter | solution.py:26
  148.8 1.4 fusion.14
  150.2 8.0 %all_gather.15 = bf16[128,3072]{1,0:T(8,128)(2,1)S(1)} all-gather(bf16[32,3072]{1,0:T(8,128)(2,1)S(1)} %get-tuple-element.16), channel_id=1, replica_groups=mesh['row'=4,'col'=8] {'row'}, dimensions={0}, use_global_device_ids=true | all-gather | bytes 983040 | tf_op jit(solution)/shard_map/all_gather | solution.py:30
  158.2 15.5 %fusion.2 = f32[128,3072]{1,0:T(8,128)} fusion(bf16[128,3072]{1,0:T(8,128)(2,1)S(1)} %all_gather.15, bf16[3072,3072]{1,0:T(8,128)(2,1)} %param.7, bf16[384,8,24,128]{3,2,1,0:T(8,128)(2,1)} %bitcast.51), kind=kOutput, calls=%fused_computation.6 | convolution fusion | flops 2425356288 | bytes 40108032 | tf_op jit(solution)/shard_map/dot_general | solution.py:20
  173.7 0.0 reduce-scatter.11.cloned.1.call-update
  173.8 0.0 reduce-scatter.9.cloned.1.call-start
  173.8 0.1 copy.24
  173.9 8.9 %all_gather.13 = bf16[128,3072]{1,0:T(8,128)(2,1)S(1)} all-gather(bf16[32,3072]{1,0:T(8,128)(2,1)S(1)} %get-tuple-element.17), channel_id=1, replica_groups=mesh['row'=4,'col'=8] {'row'}, dimensions={0}, use_global_device_ids=true | all-gather | bytes 983040 | tf_op jit(solution)/shard_map/all_gather | solution.py:30
  182.7 15.5 %fusion.5 = f32[128,3072]{1,0:T(8,128)} fusion(bf16[128,3072]{1,0:T(8,128)(2,1)S(1)} %all_gather.13, bf16[3072,3072]{1,0:T(8,128)(2,1)} %param.8, bf16[384,8,24,128]{3,2,1,0:T(8,128)(2,1)} %bitcast.49), kind=kOutput, calls=%fused_computation.9 | convolution fusion | flops 2425356288 | bytes 40108032 | tf_op jit(solution)/shard_map/dot_general | solution.py:20
  198.3 12.6 %mul.112 = f32[24,128,24,128]{1,0,3,2:T(8,128)} broadcast(f32[24,24]{0,1:T(8,128)S(1)} %copy.24), dimensions={0,2} | broadcast | bytes 37751040 | tf_op jit(solution)/shard_map/mul | solution.py:12
  210.9 26.6 %fusion.1 = bf16[3072,3072]{0,1:T(8,128)(2,1)} fusion(f32[384,8,24,128]{3,2,1,0:T(8,128)} %bitcast.46, bf16[128,3072]{1,0:T(8,128)(2,1)S(1)} %all_gather.15, bf16[128,3072]{1,0:T(8,128)(2,1)S(1)} %all_gather.12), kind=kOutput, calls=%fused_computation.3 | convolution fusion | flops 2434793472 | bytes 58195968 | tf_op jit(solution)/shard_map/dot_general | solution.py:55
  237.5 24.6 %copy.25 = bf16[3072,3072]{1,0:T(8,128)(2,1)} copy(bf16[3072,3072]{0,1:T(8,128)(2,1)} %fusion.1) | data formatting | bytes 37748736
  262.1 12.6 %mul.115 = f32[24,128,24,128]{3,2,1,0:T(8,128)} broadcast(f32[24,24]{1,0:T(8,128)S(1)} %get-tuple-element.18), dimensions={0,2} | broadcast | bytes 37751040 | tf_op jit(solution)/shard_map/mul | solution.py:12
  274.8 26.4 %fusion = bf16[3072,3072]{1,0:T(8,128)(2,1)} fusion(f32[384,8,24,128]{3,2,1,0:T(8,128)} %bitcast.47, bf16[128,3072]{1,0:T(8,128)(2,1)S(1)} %all_gather.13, bf16[128,3072]{1,0:T(8,128)(2,1)S(1)} %all_gather.14), kind=kOutput, calls=%fused_computation.1 | convolution fusion | flops 2434793472 | bytes 58195968 | tf_op jit(solution)/shard_map/dot_general | solution.py:50
  301.1 1.6 convert_element_type.39
  302.7 5.0 %reduce-scatter.9.cloned.1.call-done = f32[16,3072]{1,0:T(8,128)} async-done(((f32[128,3072]{1,0:T(8,128)}), f32[16,3072]{1,0:T(8,128)}) %reduce-scatter.9.cloned.1.call-update) | async-done | bytes 196624 | tf_op jit(solution)/shard_map/reduce_scatter | solution.py:34
  307.7 1.6 convert_element_type.37
  (7 shorter events, 0.0 us)
Async XLA Ops:
  7.2 112.6 %reduce-scatter.15.cloned.1.call-start = ((), (), s32[]{:S(2)}) async-start(), calls=%async_computation.7 | async-start | bytes 1966080 | tf_op jit(solution)/shard_map/reduce_scatter | solution.py:26
  48.9 16.1 %copy-start.1 = (s32[24,24]{1,0:T(8,128)S(1)}, s32[24,24]{1,0:T(8,128)}, u32[]{:S(2)}) copy-start(s32[24,24]{1,0:T(8,128)} %param.9) | copy-start | bytes 6916
  48.9 16.2 %copy-start = (bf16[16,3072]{1,0:T(8,128)(2,1)S(1)}, bf16[16,3072]{1,0:T(8,128)(2,1)}, u32[]{:S(2)}) copy-start(bf16[16,3072]{1,0:T(8,128)(2,1)} %param.6) | copy-start | bytes 294916
  65.0 83.8 %reduce-scatter.13.cloned.1.call-start = ((), (), s32[]{:S(2)}) async-start(), calls=%async_computation.6 | async-start | bytes 1966080 | tf_op jit(solution)/shard_map/reduce_scatter | solution.py:26
  119.7 181.4 %reduce-scatter.11.cloned.1.call-start = ((), (), s32[]{:S(2)}) async-start(), calls=%async_computation.5 | async-start | bytes 1769472 | tf_op jit(solution)/shard_map/reduce_scatter | solution.py:34
  173.8 133.9 %reduce-scatter.9.cloned.1.call-start = ((), (), s32[]{:S(2)}) async-start(), calls=%async_computation.4 | async-start | bytes 1769472 | tf_op jit(solution)/shard_map/reduce_scatter | solution.py:34
Sparse Core Ops, SparseCore 0:
  65.1 28.9 reduce-scatter.14
  119.8 28.9 reduce-scatter.12
  173.9 66.1 reduce-scatter.10
  243.3 64.3 reduce-scatter.8
where the time goes:
time: 317 us; the launch traced here: 316 us
  matrix products  112 us (35%)
  blocking collectives  83.1 us (26%)
  local copies, waits for them, and re-layouts  66.8 us (21%)
  waiting for transfers between devices  34.1 us (11%)
  between operations  13.8 us (4%)
  other arithmetic  5.35 us (2%)
    dot_general x4, matrix products, contract(): lax.dot_general(left, weight, (((1,), (dim,)), ((), ())), preferred_eleme...  59.5 us
    mul x4, local copies, waits for them, and re-layouts, apply_mask(): shaped * mask[:, None, :, None].astype(weight.dtype)  38.9 us
    all_gather x1, blocking collectives, local(): lax.all_gather(out_grad, 'col', axis=0, tiled=True)  34.1 us
    all_gather x1, blocking collectives, local(): lax.all_gather(tokens, 'col', axis=0, tiled=True)  32.1 us
    reduce_scatter x2, waiting for transfers between devices, hidden_sum(): lax.psum_scatter(contract(left, weight, dim), 'row', scatter_dimension=0,...  29 us
    unnamed x7, local copies, waits for them, and re-layouts  27.9 us
    dot_general x1, matrix products, local(): lax.dot_general(gathered, hid_all, (((0,), (0,)), ((), ())), preferred_el...  26.6 us
    dot_general x1, matrix products, local(): lax.dot_general(act_all, grad_rows, (((0,), (0,)), ((), ())), preferred_e...  26.4 us
  transfers between devices with their start and end apart: 4, of which 2 were waited for; matrix products, arithmetic and copies ran while one was open for 45% of the time, Pallas kernels for 0%

commit v1 on v0

v1 whole, which is shorter than its diff:
```python
import functools
import math

import jax
import jax.numpy as jnp
from jax import lax
from jax.experimental import pallas as pl
from jax.experimental.pallas import tpu as pltpu
from jax.sharding import PartitionSpec as P

BLK = 128
SUB = 16
MESH = pl.DeviceIdType.MESH
VMEM = pl.BlockSpec(memory_space=pltpu.VMEM)
DMA = pltpu.SemaphoreType.DMA
GELU_A, GELU_B = 0.7978845608028654, 0.044715


def remote(src, dst, send, recv, axis, device):
    return pltpu.make_async_remote_copy(
        src_ref=src, dst_ref=dst, send_sem=send, recv_sem=recv,
        device_id={axis: device}, device_id_type=MESH,
    )


def greet(axis, peers):
    barrier = pltpu.get_barrier_semaphore()
    for peer in peers:
        pl.semaphore_signal(barrier, inc=1, device_id={axis: peer}, device_id_type=MESH)
    pl.semaphore_wait(barrier, len(peers))


def gather_kernel(far, near, *refs):
    srcs, dsts, (zs, zr, ys, yr, own) = refs[:2], refs[2:4], refs[4:]
    me = lax.axis_index("col")
    z, y = me // near, lax.rem(me, near)
    along_z = [lax.rem(z + d, far) * near + y for d in range(1, far)]
    along_y = [z * near + lax.rem(y + e, near) for e in range(1, near)]
    greet("col", along_z + along_y)
    sent = []
    for a in range(2):
        for e, peer in enumerate(along_y):
            sent.append(remote(srcs[a], dsts[a].at[me], ys.at[a, 0, e], yr.at[a, 0, e], "col", peer))
            sent[-1].start()
        for d, peer in enumerate(along_z):
            sent.append(remote(srcs[a], dsts[a].at[me], zs.at[a, d], zr.at[a, d], "col", peer))
            sent[-1].start()
    kept = [pltpu.make_async_copy(srcs[a], dsts[a].at[me], own.at[a]) for a in range(2)]
    for copy in kept:
        copy.start()
    for a in range(2):
        for d in range(far - 1):
            block = lax.rem(z + far - d - 1, far) * near + y
            slot = dsts[a].at[block]
            remote(srcs[a], slot, zs.at[a, d], zr.at[a, d], "col", along_z[d]).wait_recv()
            for e, peer in enumerate(along_y):
                sent.append(remote(slot, slot, ys.at[a, d + 1, e], yr.at[a, d + 1, e], "col", peer))
                sent[-1].start()
    for a in range(2):
        for d in range(far):
            for e in range(near - 1):
                block = lax.rem(z + far - d, far) * near + lax.rem(y + near - e - 1, near)
                slot = dsts[a].at[block]
                remote(slot, slot, ys.at[a, d, e], yr.at[a, d, e], "col", along_y[e]).wait_recv()
    for copy in sent:
        copy.wait_send()
    for copy in kept:
        copy.wait()


def gather(far, near, first, second):
    out = jax.ShapeDtypeStruct((far * near,) + first.shape, first.dtype)
    gathered = pl.pallas_call(
        functools.partial(gather_kernel, far, near),
        out_shape=(out, out),
        in_specs=[VMEM, VMEM],
        out_specs=(VMEM, VMEM),
        scratch_shapes=[
            DMA((2, far - 1)), DMA((2, far - 1)),
            DMA((2, far, near - 1)), DMA((2, far, near - 1)), DMA((2,)),
        ],
        compiler_params=pltpu.CompilerParams(collective_id=0, has_side_effects=True),
        name="gather_col",
    )(first, second)
    return [each.reshape(-1, first.shape[1]) for each in gathered]


def gelu_parts(value):
    square = value * value
    tanh = jnp.tanh(GELU_A * (value + GELU_B * (square * value)))
    half = 0.5 * (1.0 + tanh)
    slope = half + 0.5 * value * (1.0 - tanh * tanh) * (GELU_A * (1.0 + (3.0 * GELU_B) * square))
    return value * half, slope


def row_kernel(chips, cores, *refs):
    parts, outs = refs[:2], refs[2:4]
    pair, sums, landed, slope, ps, pr, xs, xr, gs, gr, fs, fr = refs[4:]
    me = lax.axis_index("row")
    x, k = me // cores, lax.rem(me, cores)
    partner = x * cores + (1 - k)
    across = [lax.rem(x + d, chips) for d in range(1, chips)]
    peers = [c * cores + k for c in across]
    greet("row", [partner] + peers)
    sent = []
    for a in range(2):
        for d, c in enumerate(across + [x]):
            sent.append(remote(parts[a].at[c, 1 - k], pair.at[a, c], ps.at[a, d], pr.at[a, d], "row", partner))
            sent[-1].start()
    for a in range(2):
        for d, c in enumerate(across):
            remote(parts[a].at[c, 1 - k], pair.at[a, c], ps.at[a, d], pr.at[a, d], "row", partner).wait_recv()
            sums[a, d] = (parts[a][c, k] + pair[a, c]).astype(sums.dtype)
            sent.append(remote(sums.at[a, d], landed.at[a, d], xs.at[a, d], xr.at[a, d], "row", peers[d]))
            sent[-1].start()
    for a in range(2):
        last = chips - 1
        remote(parts[a].at[x, 1 - k], pair.at[a, x], ps.at[a, last], pr.at[a, last], "row", partner).wait_recv()
        total = parts[a][x, k] + pair[a, x]
        for d in range(chips - 1):
            remote(sums.at[a, d], landed.at[a, d], xs.at[a, d], xr.at[a, d], "row", peers[d]).wait_recv()
            total = total + landed[a, d].astype(jnp.float32)
        if a == 0:
            act, rate = gelu_parts(total)
            slope[...] = rate
            outs[a][me] = act.astype(outs[a].dtype)
        else:
            outs[a][me] = (total * slope[...]).astype(outs[a].dtype)
        mine = outs[a].at[me]
        for d, peer in enumerate(peers):
            sent.append(remote(mine, mine, gs.at[a, d], gr.at[a, d], "row", peer))
            sent[-1].start()
        sent.append(remote(mine, mine, fs.at[a, chips - 1], fr.at[a, chips - 1], "row", partner))
        sent[-1].start()
    for a in range(2):
        for d in range(chips - 1):
            slot = outs[a].at[lax.rem(x + chips - d - 1, chips) * cores + k]
            remote(slot, slot, gs.at[a, d], gr.at[a, d], "row", peers[d]).wait_recv()
            sent.append(remote(slot, slot, fs.at[a, d], fr.at[a, d], "row", partner))
            sent[-1].start()
    for a in range(2):
        for d in range(chips):
            slot = outs[a].at[lax.rem(x + chips - lax.rem(d + 1, chips), chips) * cores + (1 - k)]
            remote(slot, slot, fs.at[a, d], fr.at[a, d], "row", partner).wait_recv()
    for copy in sent:
        copy.wait_send()


def row_exchange(chips, cores, first, second):
    tokens, width = first.shape
    share = tokens // (chips * cores)
    out = jax.ShapeDtypeStruct((chips * cores, share, width), jnp.bfloat16)
    shaped = (chips, cores, share, width)
    gathered = pl.pallas_call(
        functools.partial(row_kernel, chips, cores),
        out_shape=(out, out),
        in_specs=[VMEM, VMEM],
        out_specs=(VMEM, VMEM),
        scratch_shapes=[
            pltpu.VMEM((2, chips, share, width), jnp.float32),
            pltpu.VMEM((2, chips - 1, share, width), jnp.bfloat16),
            pltpu.VMEM((2, chips - 1, share, width), jnp.bfloat16),
            pltpu.VMEM((share, width), jnp.float32),
            DMA((2, chips)), DMA((2, chips)),
            DMA((2, chips - 1)), DMA((2, chips - 1)),
            DMA((2, chips - 1)), DMA((2, chips - 1)),
            DMA((2, chips)), DMA((2, chips)),
        ],
        compiler_params=pltpu.CompilerParams(collective_id=1, has_side_effects=True),
        name="row_exchange",
    )(first.reshape(shaped), second.reshape(shaped))
    return [each.reshape(tokens, width) for each in gathered]


def column_kernel(far, near, pieces, *refs):
    wide, short, outs = refs[:2], refs[2:4], refs[4:6]
    across, sums, landed, ys, yr, zs, zr = refs[6:]
    me = lax.axis_index("col")
    z, y = me // near, lax.rem(me, near)
    rows_y = [lax.rem(y + e, near) for e in range(1, near)]
    rows_z = [lax.rem(z + d, far) for d in range(1, far)]
    peers_y = [z * near + e for e in rows_y]
    peers_z = [d * near + y for d in rows_z]
    greet("col", peers_y + peers_z)
    width = outs[0].shape[-1] // pieces
    steps = [(a, p) for a in range(2) for p in range(pieces)]
    cut = lambda p: pl.ds(p * width, width)
    sent = []

    def over_y(i, e):
        a, p = steps[i]
        return remote(short[a].at[:, rows_y[e], :, cut(p)], across.at[i, e], ys.at[i, e], yr.at[i, e], "col", peers_y[e])

    def over_z(i, d):
        return remote(sums.at[i, d], landed.at[i, d], zs.at[i, d], zr.at[i, d], "col", peers_z[d])

    def pair_sum(i, row):
        a, p = steps[i]
        total = wide[a][row, y, :, cut(p)]
        for e in range(near - 1):
            total = total + across[i, e, row].astype(jnp.float32)
        return total

    for i in range(len(steps)):
        for e in range(near - 1):
            sent.append(over_y(i, e))
            sent[-1].start()
    for i in range(len(steps)):
        for e in range(near - 1):
            over_y(i, e).wait_recv()
        for d in range(far - 1):
            sums[i, d] = pair_sum(i, rows_z[d]).astype(sums.dtype)
            sent.append(over_z(i, d))
            sent[-1].start()
    for i, (a, p) in enumerate(steps):
        total = pair_sum(i, z)
        for d in range(far - 1):
            over_z(i, d).wait_recv()
            total = total + landed[i, d].astype(jnp.float32)
        outs[a][:, cut(p)] = total.astype(outs[a].dtype)
    for copy in sent:
        copy.wait_send()


def column_sums(far, near, wide, short):
    tokens, width = wide[0].shape
    share = tokens // (far * near)
    pieces = 2
    cols = width // pieces
    out = jax.ShapeDtypeStruct((share, width), jnp.bfloat16)
    shaped = (far, near, share, width)
    count = 2 * pieces
    return pl.pallas_call(
        functools.partial(column_kernel, far, near, pieces),
        out_shape=(out, out),
        in_specs=[VMEM] * 4,
        out_specs=(VMEM, VMEM),
        scratch_shapes=[
            pltpu.VMEM((count, near - 1, far, share, cols), jnp.bfloat16),
            pltpu.VMEM((count, far - 1, share, cols), jnp.bfloat16),
            pltpu.VMEM((count, far - 1, share, cols), jnp.bfloat16),
            DMA((count, near - 1)), DMA((count, near - 1)),
            DMA((count, far - 1)), DMA((count, far - 1)),
        ],
        compiler_params=pltpu.CompilerParams(collective_id=2, has_side_effects=True),
        name="column_sums",
    )(*[each.reshape(shaped) for each in (*wide, *short)])


def masked(weight, flags):
    rows, cols = weight.shape
    shaped = weight.reshape(rows // BLK, BLK // SUB, SUB, cols)
    return (shaped * flags.reshape(rows // BLK, 1, SUB, cols)).reshape(rows, cols)


def products_kernel(left_ref, right_ref, down_ref, down_flags, up_ref, up_flags, *outs):
    ahead = jnp.dot(left_ref[...], masked(down_ref[...], down_flags[...]), preferred_element_type=jnp.float32)
    back = lax.dot_general(
        right_ref[...], masked(up_ref[...], up_flags[...]),
        (((1,), (1,)), ((), ())), preferred_element_type=jnp.float32,
    )
    outs[0][...], outs[1][...] = ahead, back
    if len(outs) > 2:
        outs[2][...], outs[3][...] = ahead.astype(outs[2].dtype), back.astype(outs[3].dtype)


def products(left, right, down, down_flags, up, up_flags, short):
    tokens, depth = left.shape
    width = down.shape[1]
    tile = 2 * BLK if width % (2 * BLK) == 0 else BLK
    per = tile // BLK * SUB
    whole = lambda each: pl.BlockSpec(each.shape, lambda i: (0, 0))
    kinds = [jnp.float32] * 2 + [jnp.bfloat16] * (2 if short else 0)
    return pl.pallas_call(
        products_kernel,
        grid=(width // tile,),
        out_shape=[jax.ShapeDtypeStruct((tokens, width), kind) for kind in kinds],
        in_specs=[
            whole(left), whole(right),
            pl.BlockSpec((depth, tile), lambda i: (0, i)),
            pl.BlockSpec((depth // BLK * SUB, tile), lambda i: (0, i)),
            pl.BlockSpec((tile, depth), lambda i: (i, 0)),
            pl.BlockSpec((per, depth), lambda i: (i, 0)),
        ],
        out_specs=[pl.BlockSpec((tokens, tile), lambda i: (0, i))] * len(kinds),
        name="products",
    )(left, right, down, down_flags, up, up_flags)


def outer_kernel(tokens_ref, hid_ref, in_flags, act_ref, grad_ref, out_flags, in_ref, out_ref):
    def one(left, right, flags, out):
        full = lax.dot_general(left, right, (((0,), (0,)), ((), ())), preferred_element_type=jnp.float32)
        out[...] = masked(full.astype(out.dtype), flags)

    one(tokens_ref[...], hid_ref[...], in_flags[...], in_ref)
    one(act_ref[...], grad_ref[...], out_flags[...], out_ref)


def outers(tokens, hid, in_flags, act, grad, out_flags):
    count, depth = tokens.shape
    width = hid.shape[1]
    steps = math.gcd(depth // BLK, width // BLK)
    steps = steps // 2 if steps % 2 == 0 else steps
    down, up = depth // steps, width // steps
    whole = lambda each: pl.BlockSpec(each.shape, lambda i: (0, 0))
    return pl.pallas_call(
        outer_kernel,
        grid=(steps,),
        out_shape=[
            jax.ShapeDtypeStruct((depth, width), jnp.bfloat16),
            jax.ShapeDtypeStruct((width, depth), jnp.bfloat16),
        ],
        in_specs=[
            pl.BlockSpec((count, down), lambda i: (0, i)), whole(hid),
            pl.BlockSpec((down // BLK * SUB, width), lambda i: (i, 0)),
            pl.BlockSpec((count, up), lambda i: (0, i)), whole(grad),
            pl.BlockSpec((up // BLK * SUB, depth), lambda i: (i, 0)),
        ],
        out_specs=[
            pl.BlockSpec((down, width), lambda i: (i, 0)),
            pl.BlockSpec((up, depth), lambda i: (i, 0)),
        ],
        name="outers",
    )(tokens, hid, in_flags, act, grad, out_flags)


def spread(mask):
    rows, cols = mask.shape
    flags = mask.astype(jnp.bfloat16)[:, None, :, None]
    return jnp.broadcast_to(flags, (rows, SUB, cols, BLK)).reshape(rows * SUB, cols * BLK)


def local(far, near, chips, cores, tokens, w_in, w_out, mask_in, mask_out, out_grad):
    in_flags, out_flags = spread(mask_in), spread(mask_out)
    gathered, grad_rows = gather(far, near, tokens, out_grad)
    hidden, act_grad = products(gathered, grad_rows, w_in, in_flags, w_out, out_flags, False)
    act, hid = row_exchange(chips, cores, hidden, act_grad)
    sums = products(act, hid, w_out, out_flags, w_in, in_flags, True)
    mixed, tokens_grad = column_sums(far, near, sums[:2], sums[2:])
    w_in_grad, w_out_grad = outers(gathered, hid, in_flags, act, grad_rows, out_flags)
    return (mixed, tokens_grad, w_in_grad, w_out_grad)


def solution(mesh):
    columns, rows = mesh.shape["col"], mesh.shape["row"]
    near = 2 ** (int(math.log2(columns)) // 2)
    return jax.shard_map(
        functools.partial(local, columns // near, near, rows // 2, 2),
        mesh=mesh,
        in_specs=(
            P("col", "row"),
            P("row", "col"),
            P("col", "row"),
            P("row", "col"),
            P("col", "row"),
            P("col", "row"),
        ),
        out_specs=(P("col", "row"), P("col", "row"), P("row", "col"), P("col", "row")),
        check_vma=False,
    )
```

time: 317 us -> 155 us (0.49)
  Pallas kernels: 0 us -> 147 us
  matrix products: 112 us -> 0 us
  blocking collectives: 83.1 us -> 0 us
  local copies, waits for them, and re-layouts: 66.8 us -> 5.32 us
  waiting for transfers between devices: 34.1 us -> 0 us
  between operations: 13.8 us -> 0.69 us
  other arithmetic: 5.35 us -> 1.42 us
    pallas_call x0 -> x6, Pallas kernels: none -> 147 us  [the longest x2 41.4 us: products(): pl.pallas_call(products_kernel, grid=(width // tile,), out_shape=[jax.Sha...]
    dot_general x6 -> x0, matrix products: 112 us -> none  [the longest x4 59.5 us: contract(): lax.dot_general(left, weight, (((1,), (dim,)), ((), ())), preferred_eleme...]
    all_gather x4 -> x0, blocking collectives: 83.1 us -> none  [the longest x1 34.1 us: local(): lax.all_gather(out_grad, 'col', axis=0, tiled=True)]
    mul x4 -> x0, local copies, waits for them, and re-layouts: 38.9 us -> none  [apply_mask(): shaped * mask[:, None, :, None].astype(weight.dtype)]
    reduce_scatter x4 -> x0, waiting for transfers between devices: 34 us -> none  [the longest x2 29 us: hidden_sum(): lax.psum_scatter(contract(left, weight, dim), 'row', scatter_dimension=0,...]
    unnamed x7 -> x6, local copies, waits for them, and re-layouts: 27.9 us -> 1.29 us
    convert_element_type x5 -> x2, other arithmetic: 5.35 us -> 1.42 us  [spread(): flags = mask.astype(jnp.bfloat16)[:, None, :, None]]
    reshape x0 -> x1, local copies, waits for them, and re-layouts: none -> 3.29 us  [spread(): jnp.broadcast_to(flags, (rows, SUB, cols, BLK))]
  transfers between devices with their start and end apart: 4 -> 0, of which waited for: 2 -> 0; matrix products, arithmetic and copies ran while one was open for 45% -> 0% of each run, Pallas kernels for 0% -> 0%
where the time goes in v1:
time: 155 us; the launch traced here: 154 us
  Pallas kernels  147 us (95%)
  local copies, waits for them, and re-layouts  5.32 us (3%)
    pallas_call x2, Pallas kernels, products(): pl.pallas_call(products_kernel, grid=(width // tile,), out_shape=[jax.Sha...  41.4 us
    pallas_call x1, Pallas kernels, column_sums(): pl.pallas_call(functools.partial(column_kernel, far, near, pieces), out_s...  31.6 us
    pallas_call x1, Pallas kernels, gather(): pl.pallas_call(functools.partial(gather_kernel, far, near), out_shape=(ou...  29.7 us
    pallas_call x1, Pallas kernels, row_exchange(): pl.pallas_call(functools.partial(row_kernel, chips, cores), out_shape=(ou...  25.8 us
    pallas_call x1, Pallas kernels, outers(): pl.pallas_call(outer_kernel, grid=(steps,), out_shape=[jax.ShapeDtypeStru...  18.4 us
    reshape x1, local copies, waits for them, and re-layouts, spread(): jnp.broadcast_to(flags, (rows, SUB, cols, BLK))  3.29 us

profile of v1, /device:TPU:0, one launch (start us, length us, event | category | flops | bytes accessed | tf_op | source)
XLA Modules:
  0.0 154.4 jit_solution(2027855827743204019)
XLA Ops:
  0.6 0.7 convert_element_type.6
  1.3 0.7 convert_element_type.7
  2.1 29.7 %gather_col.1 = (bf16[8,16,3072]{2,1,0:T(8,128)(2,1)}, bf16[8,16,3072]{2,1,0:T(8,128)(2,1)}) custom-call(bf16[16,3072]{1,0:T(8,128)(2,1)} %refs_0_.1, bf16[16,3072]{1,0:T(8,128)(2,1)} %refs_1_.1), custom_call_target="tpu_custom_call" | custom-call | tf_op jit(solution)/shard_map/gather_col/pallas_call | solution.py:73
  31.8 0.4 broadcast_in_dim.5
  32.2 0.4 broadcast_in_dim.4
  32.5 3.3 %copy_bitcast_fusion = (bf16[384,3072]{1,0:T(8,128)(2,1)}, bf16[384,3072]{1,0:T(8,128)(2,1)}) fusion(bf16[48,8,24,128]{3,2,1,0:T(8,128)(2,1)S(1)} %bitcast.18, bf16[48,8,24,128]{3,2,1,0:T(8,128)(2,1)S(1)} %bitcast.19), kind=kLoop, calls=%fused_computation | loop fusion | bytes 9437184 | tf_op jit(solution)/shard_map/reshape | solution.py:330
  35.8 20.5 %products.2 = (f32[128,3072]{1,0:T(8,128)}, f32[128,3072]{1,0:T(8,128)}) custom-call(bf16[128,3072]{1,0:T(8,128)(2,1)} %bitcast.20, bf16[128,3072]{1,0:T(8,128)(2,1)} %bitcast.22, bf16[3072,3072]{1,0:T(8,128)(2,1)} %up_ref.3, bf16[384,3072]{1,0:T(8,128)(2,1)} %get-tuple-element.33.down_flags.up_flags.in_flags, bf16[3072,3072]{1,0:T(8,128)(2,1)} %down_ref.3, ...), custom_call_target="tpu_custom_call" | custom-call | tf_op jit(solution)/shard_map/products/pallas_call | solution.py:274
  56.4 25.8 %row_exchange.1 = (bf16[4,32,3072]{2,1,0:T(8,128)(2,1)}, bf16[4,32,3072]{2,1,0:T(8,128)(2,1)}) custom-call(f32[2,2,32,3072]{3,2,1,0:T(8,128)} %bitcast.28, f32[2,2,32,3072]{3,2,1,0:T(8,128)} %bitcast.29), custom_call_target="tpu_custom_call" | custom-call | tf_op jit(solution)/shard_map/row_exchange/pallas_call | solution.py:154
  82.2 20.9 %products.3 = (f32[128,3072]{1,0:T(8,128)}, f32[128,3072]{1,0:T(8,128)}, bf16[128,3072]{1,0:T(8,128)(2,1)}, bf16[128,3072]{1,0:T(8,128)(2,1)}) custom-call(bf16[128,3072]{1,0:T(8,128)(2,1)} %bitcast.24, bf16[128,3072]{1,0:T(8,128)(2,1)} %bitcast.26, bf16[3072,3072]{1,0:T(8,128)(2,1)} %down_ref.3, ...), custom_call_target="tpu_custom_call" | custom-call | tf_op jit(solution)/shard_map/products/pallas_call | solution.py:274
  103.1 31.6 %column_sums.1 = (bf16[16,3072]{1,0:T(8,128)(2,1)}, bf16[16,3072]{1,0:T(8,128)(2,1)}) custom-call(f32[4,2,16,3072]{3,2,1,0:T(8,128)} %bitcast.30, f32[4,2,16,3072]{3,2,1,0:T(8,128)} %bitcast.31, bf16[4,2,16,3072]{3,2,1,0:T(8,128)(2,1)} %bitcast.32, bf16[4,2,16,3072]{3,2,1,0:T(8,128)(2,1)} %bitcast.33), custom_call_target="tpu_custom_call" | custom-call | tf_op jit(solution)/shard_map/column_sums/pallas_call | solution.py:233
  134.7 0.0 copy-start.1
  134.7 0.0 copy-start
  134.7 18.4 %outers.1 = (bf16[3072,3072]{1,0:T(8,128)(2,1)}, bf16[3072,3072]{1,0:T(8,128)(2,1)}) custom-call(bf16[128,3072]{1,0:T(8,128)(2,1)} %bitcast.21, bf16[128,3072]{1,0:T(8,128)(2,1)} %bitcast.27, bf16[384,3072]{1,0:T(8,128)(2,1)} %get-tuple-element.33.down_flags.up_flags.in_flags, bf16[128,3072]{1,0:T(8,128)(2,1)} %bitcast.25, bf16[128,3072]{1,0:T(8,128)(2,1)} %bitcast.23, ...), custom_call_target="tpu_custom_call" | custom-call | tf_op jit(solution)/shard_map/outers/pallas_call | solution.py:306
  153.1 0.0 copy-done.1
  153.1 0.6 copy.16
  153.7 0.0 copy-done
  153.7 0.6 copy.17
Async XLA Ops:
  134.7 18.4 %copy-start.1 = (bf16[16,3072]{1,0:T(8,128)(2,1)S(1)}, bf16[16,3072]{1,0:T(8,128)(2,1)}, u32[]{:S(2)}) copy-start(bf16[16,3072]{1,0:T(8,128)(2,1)} %get-tuple-element.38) | copy-start | bytes 294916
  134.7 19.0 %copy-start = (bf16[16,3072]{1,0:T(8,128)(2,1)S(1)}, bf16[16,3072]{1,0:T(8,128)(2,1)}, u32[]{:S(2)}) copy-start(bf16[16,3072]{1,0:T(8,128)(2,1)} %get-tuple-element.39) | copy-start | bytes 294916

commit v2 on v1

v2 whole, which is shorter than its diff:
```python
import functools
import math

import jax
import jax.numpy as jnp
from jax import lax
from jax.experimental import pallas as pl
from jax.experimental.pallas import tpu as pltpu
from jax.sharding import PartitionSpec as P

BLK = 128
SUB = 16
MESH = pl.DeviceIdType.MESH
VMEM = pl.BlockSpec(memory_space=pltpu.VMEM)
DMA = pltpu.SemaphoreType.DMA
GELU_A, GELU_B = 0.7978845608028654, 0.044715


def remote(src, dst, send, recv, axis, device):
    return pltpu.make_async_remote_copy(
        src_ref=src, dst_ref=dst, send_sem=send, recv_sem=recv,
        device_id={axis: device}, device_id_type=MESH,
    )


def greet(axis, peers):
    barrier = pltpu.get_barrier_semaphore()
    for peer in peers:
        pl.semaphore_signal(barrier, inc=1, device_id={axis: peer}, device_id_type=MESH)
    pl.semaphore_wait(barrier, len(peers))


def gather_kernel(far, near, *refs):
    srcs, masks, dsts, flags, (zs, zr, ys, yr, own) = refs[:2], refs[2:4], refs[4:6], refs[6:8], refs[8:]
    me = lax.axis_index("col")
    z, y = me // near, lax.rem(me, near)
    along_z = [lax.rem(z + d, far) * near + y for d in range(1, far)]
    along_y = [z * near + lax.rem(y + e, near) for e in range(1, near)]
    greet("col", along_z + along_y)
    sent = []
    for a in range(2):
        for e, peer in enumerate(along_y):
            sent.append(remote(srcs[a], dsts[a].at[me], ys.at[a, 0, e], yr.at[a, 0, e], "col", peer))
            sent[-1].start()
        for d, peer in enumerate(along_z):
            sent.append(remote(srcs[a], dsts[a].at[me], zs.at[a, d], zr.at[a, d], "col", peer))
            sent[-1].start()
    kept = [pltpu.make_async_copy(srcs[a], dsts[a].at[me], own.at[a]) for a in range(2)]
    for copy in kept:
        copy.start()
    for a in range(2):
        flags[a][...] = spread(masks[a][...])
    for a in range(2):
        for d in range(far - 1):
            block = lax.rem(z + far - d - 1, far) * near + y
            slot = dsts[a].at[block]
            remote(srcs[a], slot, zs.at[a, d], zr.at[a, d], "col", along_z[d]).wait_recv()
            for e, peer in enumerate(along_y):
                sent.append(remote(slot, slot, ys.at[a, d + 1, e], yr.at[a, d + 1, e], "col", peer))
                sent[-1].start()
    for a in range(2):
        for d in range(far):
            for e in range(near - 1):
                block = lax.rem(z + far - d, far) * near + lax.rem(y + near - e - 1, near)
                slot = dsts[a].at[block]
                remote(slot, slot, ys.at[a, d, e], yr.at[a, d, e], "col", along_y[e]).wait_recv()
    for copy in sent:
        copy.wait_send()
    for copy in kept:
        copy.wait()


def gather(far, near, first, second, masks):
    out = jax.ShapeDtypeStruct((far * near,) + first.shape, first.dtype)
    spreads = tuple(
        jax.ShapeDtypeStruct((each.shape[0] * SUB, each.shape[1] * BLK), jnp.bfloat16) for each in masks
    )
    *gathered, in_flags, out_flags = pl.pallas_call(
        functools.partial(gather_kernel, far, near),
        out_shape=(out, out) + spreads,
        in_specs=[VMEM] * 4,
        out_specs=(VMEM,) * 4,
        scratch_shapes=[
            DMA((2, far - 1)), DMA((2, far - 1)),
            DMA((2, far, near - 1)), DMA((2, far, near - 1)), DMA((2,)),
        ],
        compiler_params=pltpu.CompilerParams(collective_id=0, has_side_effects=True),
        name="gather_col",
    )(first, second, *masks)
    return [each.reshape(-1, first.shape[1]) for each in gathered] + [in_flags, out_flags]


def spread(mask):
    rows, cols = mask.shape

    def repeats(shape, dim, size):
        apart = lax.broadcasted_iota(jnp.int32, shape, dim) - size * lax.broadcasted_iota(jnp.int32, shape, 1 - dim)
        return jnp.where((apart >= 0) & (apart < size), 1.0, 0.0).astype(jnp.bfloat16)

    flags = mask.astype(jnp.float32).astype(jnp.bfloat16)
    tall = jnp.dot(repeats((rows * SUB, rows), 0, SUB), flags, preferred_element_type=jnp.float32)
    wide = jnp.dot(tall.astype(jnp.bfloat16), repeats((cols, cols * BLK), 1, BLK), preferred_element_type=jnp.float32)
    return wide.astype(jnp.bfloat16)


def masked(weight, flags):
    rows, cols = weight.shape
    shaped = weight.reshape(rows // BLK, BLK // SUB, SUB, cols)
    return (shaped * flags.reshape(rows // BLK, 1, SUB, cols)).reshape(rows, cols)


def tiling(width):
    tile = 2 * BLK if width % (2 * BLK) == 0 else BLK
    tiles = width // tile
    pieces = next(count for count in (4, 3, 2, 1) if tiles % count == 0)
    return tile, tiles, pieces


def stream_shapes(depth, tile):
    return [
        pltpu.VMEM((2, depth, tile), jnp.bfloat16), pltpu.VMEM((2, depth // BLK * SUB, tile), jnp.bfloat16),
        pltpu.VMEM((2, tile, depth), jnp.bfloat16), pltpu.VMEM((2, tile // BLK * SUB, depth), jnp.bfloat16),
        DMA((4, 2)),
    ]


def streamed(tile, tiles, left, right, sources, buffers):
    *slots, arrived = buffers
    rows = tile // BLK * SUB

    def copies(t):
        slot = lax.rem(t, 2)
        across = pl.ds(pl.multiple_of(t * tile, tile), tile)
        down = pl.ds(pl.multiple_of(t * rows, rows), rows)
        views = [sources[0].at[:, across], sources[1].at[:, across], sources[2].at[across, :], sources[3].at[down, :]]
        return [pltpu.make_async_copy(view, slots[n].at[slot], arrived.at[n, slot]) for n, view in enumerate(views)]

    def first():
        for copy in copies(0):
            copy.start()

    def pair(t):
        for copy in copies(t):
            copy.wait()

        @pl.when(t + 1 < tiles)
        def _():
            for copy in copies(t + 1):
                copy.start()

        slot = lax.rem(t, 2)
        ahead = jnp.dot(left[...], masked(slots[0][slot], slots[1][slot]), preferred_element_type=jnp.float32)
        back = lax.dot_general(
            right[...], masked(slots[2][slot], slots[3][slot]),
            (((1,), (1,)), ((), ())), preferred_element_type=jnp.float32,
        )
        return ahead, back

    return first, pair


def gelu_parts(value):
    square = value * value
    tanh = jnp.tanh(GELU_A * (value + GELU_B * (square * value)))
    half = 0.5 * (1.0 + tanh)
    slope = half + 0.5 * value * (1.0 - tanh * tanh) * (GELU_A * (1.0 + (3.0 * GELU_B) * square))
    return value * half, slope


def row_kernel(chips, cores, tile, tiles, pieces, left, right, *refs):
    sources, outs, refs = refs[:4], refs[4:6], refs[6:]
    buffers, refs = refs[:5], refs[5:]
    parts, pair, sums, landed, ps, pr, xs, xr, gs, gr, fs, fr = refs
    me = lax.axis_index("row")
    x, k = me // cores, lax.rem(me, cores)
    partner = x * cores + (1 - k)
    across = [lax.rem(x + d, chips) for d in range(1, chips)]
    peers = [c * cores + k for c in across]
    first, multiply = streamed(tile, tiles, left, right, sources, buffers)
    first()
    greet("row", [partner] + peers)
    per = tiles // pieces
    cols = per * tile
    shaped = parts.shape[2:5]
    sent = []

    def push(copy):
        copy.start()
        sent.append(copy)

    def to_partner(a, p):
        return remote(parts.at[a, p, :, 1 - k], pair.at[a, p], ps.at[a, p], pr.at[a, p], "row", partner)

    def to_chip(a, p, d):
        return remote(sums.at[a, p, d], landed.at[a, p, d], xs.at[a, p, d], xr.at[a, p, d], "row", peers[d])

    def share(a, p, owner):
        return outs[a].at[owner, :, pl.ds(p * cols, cols)]

    def give_chip(a, p, d, owner):
        return remote(share(a, p, owner), share(a, p, owner), gs.at[a, p, d], gr.at[a, p, d], "row", peers[d])

    def give_partner(a, p, d, owner):
        return remote(share(a, p, owner), share(a, p, owner), fs.at[a, p, d], fr.at[a, p, d], "row", partner)

    def compute(p):
        def step(j, carry):
            spot = pl.ds(pl.multiple_of(j * tile, tile), tile)
            for a, value in enumerate(multiply(p * per + j)):
                parts[a, p, :, :, :, spot] = value.reshape(*shaped, tile)
            return carry

        lax.fori_loop(0, per, step, 0)
        for a in range(2):
            push(to_partner(a, p))

    def reduce_pair(p):
        for a in range(2):
            to_partner(a, p).wait_recv()
            for d, c in enumerate(across):
                sums[a, p, d] = (parts[a, p, c, k] + pair[a, p, c]).astype(sums.dtype)
                push(to_chip(a, p, d))

    def finish(p):
        totals = []
        for a in range(2):
            total = parts[a, p, x, k] + pair[a, p, x]
            for d in range(chips - 1):
                to_chip(a, p, d).wait_recv()
                total = total + landed[a, p, d].astype(jnp.float32)
            totals.append(total)
        act, slope = gelu_parts(totals[0])
        for a, value in enumerate((act, totals[1] * slope)):
            outs[a][me, :, pl.ds(p * cols, cols)] = value.astype(outs[a].dtype)
            for d in range(chips - 1):
                push(give_chip(a, p, d, me))
            push(give_partner(a, p, chips - 1, me))

    def forward(p):
        for a in range(2):
            for d in range(chips - 1):
                owner = lax.rem(x + chips - d - 1, chips) * cores + k
                give_chip(a, p, d, owner).wait_recv()
                push(give_partner(a, p, d, owner))

    stages = (compute, reduce_pair, finish, forward)
    for step in range(pieces + len(stages) - 1):
        for lag, stage in enumerate(stages):
            if 0 <= step - lag < pieces:
                stage(step - lag)
    for p in range(pieces):
        for a in range(2):
            for d in range(chips):
                owner = lax.rem(x + chips - lax.rem(d + 1, chips), chips) * cores + (1 - k)
                give_partner(a, p, d, owner).wait_recv()
    for copy in sent:
        copy.wait_send()


ANY = pl.BlockSpec(memory_space=pl.ANY)


def row_stage(chips, cores, left, right, down, down_flags, up, up_flags):
    tokens, depth = left.shape
    width = down.shape[1]
    tile, tiles, pieces = tiling(width)
    cols = width // pieces
    share = tokens // (chips * cores)
    out = jax.ShapeDtypeStruct((chips * cores, share, width), jnp.bfloat16)
    gathered = pl.pallas_call(
        functools.partial(row_kernel, chips, cores, tile, tiles, pieces),
        out_shape=(out, out),
        in_specs=[VMEM] * 2 + [ANY] * 4,
        out_specs=(VMEM, VMEM),
        scratch_shapes=stream_shapes(depth, tile) + [
            pltpu.VMEM((2, pieces, chips, cores, share, cols), jnp.float32),
            pltpu.VMEM((2, pieces, chips, share, cols), jnp.float32),
            pltpu.VMEM((2, pieces, chips - 1, share, cols), jnp.bfloat16),
            pltpu.VMEM((2, pieces, chips - 1, share, cols), jnp.bfloat16),
            DMA((2, pieces)), DMA((2, pieces)),
            DMA((2, pieces, chips - 1)), DMA((2, pieces, chips - 1)),
            DMA((2, pieces, chips - 1)), DMA((2, pieces, chips - 1)),
            DMA((2, pieces, chips)), DMA((2, pieces, chips)),
        ],
        compiler_params=pltpu.CompilerParams(collective_id=1, has_side_effects=True),
        name="row_stage",
    )(left, right, down, down_flags, up, up_flags)
    return [each.reshape(tokens, width) for each in gathered]


def column_kernel(far, near, tile, tiles, pieces, left, right, *refs):
    sources, outs, refs = refs[:4], refs[4:6], refs[6:]
    buffers, refs = refs[:5], refs[5:]
    wide, short, across, sums, landed, ys, yr, zs, zr = refs
    me = lax.axis_index("col")
    z, y = me // near, lax.rem(me, near)
    rows_y = [lax.rem(y + e, near) for e in range(1, near)]
    rows_z = [lax.rem(z + d, far) for d in range(1, far)]
    peers_y = [z * near + e for e in rows_y]
    peers_z = [d * near + y for d in rows_z]
    first, multiply = streamed(tile, tiles, left, right, sources, buffers)
    first()
    greet("col", peers_y + peers_z)
    per = tiles // pieces
    cols = per * tile
    shaped = wide.shape[2:5]
    sent = []

    def push(copy):
        copy.start()
        sent.append(copy)

    def over_y(a, p, e):
        return remote(short.at[a, p, :, rows_y[e]], across.at[a, p, e], ys.at[a, p, e], yr.at[a, p, e], "col", peers_y[e])

    def over_z(a, p, d):
        return remote(sums.at[a, p, d], landed.at[a, p, d], zs.at[a, p, d], zr.at[a, p, d], "col", peers_z[d])

    def near_sum(a, p, row):
        total = wide[a, p, row, y]
        for e in range(near - 1):
            total = total + across[a, p, e, row].astype(jnp.float32)
        return total

    def compute(p):
        def step(j, carry):
            spot = pl.ds(pl.multiple_of(j * tile, tile), tile)
            for a, value in enumerate(multiply(p * per + j)):
                laid = value.reshape(*shaped, tile)
                wide[a, p, :, :, :, spot] = laid
                short[a, p, :, :, :, spot] = laid.astype(short.dtype)
            return carry

        lax.fori_loop(0, per, step, 0)
        for a in range(2):
            for e in range(near - 1):
                push(over_y(a, p, e))

    def reduce_near(p):
        for a in range(2):
            for e in range(near - 1):
                over_y(a, p, e).wait_recv()
            for d in range(far - 1):
                sums[a, p, d] = near_sum(a, p, rows_z[d]).astype(sums.dtype)
                push(over_z(a, p, d))

    def finish(p):
        for a in range(2):
            total = near_sum(a, p, z)
            for d in range(far - 1):
                over_z(a, p, d).wait_recv()
                total = total + landed[a, p, d].astype(jnp.float32)
            outs[a][:, pl.ds(p * cols, cols)] = total.astype(outs[a].dtype)

    stages = (compute, reduce_near, finish)
    for step in range(pieces + len(stages) - 1):
        for lag, stage in enumerate(stages):
            if 0 <= step - lag < pieces:
                stage(step - lag)
    for copy in sent:
        copy.wait_send()


def column_stage(far, near, left, right, down, down_flags, up, up_flags):
    tokens, depth = left.shape
    width = down.shape[1]
    tile, tiles, pieces = tiling(width)
    cols = width // pieces
    share = tokens // (far * near)
    out = jax.ShapeDtypeStruct((share, width), jnp.bfloat16)
    return pl.pallas_call(
        functools.partial(column_kernel, far, near, tile, tiles, pieces),
        out_shape=(out, out),
        in_specs=[VMEM] * 2 + [ANY] * 4,
        out_specs=(VMEM, VMEM),
        scratch_shapes=stream_shapes(depth, tile) + [
            pltpu.VMEM((2, pieces, far, near, share, cols), jnp.float32),
            pltpu.VMEM((2, pieces, far, near, share, cols), jnp.bfloat16),
            pltpu.VMEM((2, pieces, near - 1, far, share, cols), jnp.bfloat16),
            pltpu.VMEM((2, pieces, far - 1, share, cols), jnp.bfloat16),
            pltpu.VMEM((2, pieces, far - 1, share, cols), jnp.bfloat16),
            DMA((2, pieces, near - 1)), DMA((2, pieces, near - 1)),
            DMA((2, pieces, far - 1)), DMA((2, pieces, far - 1)),
        ],
        compiler_params=pltpu.CompilerParams(collective_id=2, has_side_effects=True),
        name="column_stage",
    )(left, right, down, down_flags, up, up_flags)


def outer_kernel(tokens_ref, hid_ref, in_flags, act_ref, grad_ref, out_flags, in_ref, out_ref):
    def one(left, right, flags, out):
        full = lax.dot_general(left, right, (((0,), (0,)), ((), ())), preferred_element_type=jnp.float32)
        out[...] = masked(full.astype(out.dtype), flags)

    one(tokens_ref[...], hid_ref[...], in_flags[...], in_ref)
    one(act_ref[...], grad_ref[...], out_flags[...], out_ref)


def outers(tokens, hid, in_flags, act, grad, out_flags):
    count, depth = tokens.shape
    width = hid.shape[1]
    steps = math.gcd(depth // BLK, width // BLK)
    steps = steps // 2 if steps % 2 == 0 else steps
    down, up = depth // steps, width // steps
    whole = lambda each: pl.BlockSpec(each.shape, lambda i: (0, 0))
    return pl.pallas_call(
        outer_kernel,
        grid=(steps,),
        out_shape=[
            jax.ShapeDtypeStruct((depth, width), jnp.bfloat16),
            jax.ShapeDtypeStruct((width, depth), jnp.bfloat16),
        ],
        in_specs=[
            pl.BlockSpec((count, down), lambda i: (0, i)), whole(hid),
            pl.BlockSpec((down // BLK * SUB, width), lambda i: (i, 0)),
            pl.BlockSpec((count, up), lambda i: (0, i)), whole(grad),
            pl.BlockSpec((up // BLK * SUB, depth), lambda i: (i, 0)),
        ],
        out_specs=[
            pl.BlockSpec((down, width), lambda i: (i, 0)),
            pl.BlockSpec((up, depth), lambda i: (i, 0)),
        ],
        name="outers",
    )(tokens, hid, in_flags, act, grad, out_flags)


def local(far, near, chips, cores, tokens, w_in, w_out, mask_in, mask_out, out_grad):
    gathered, grad_rows, in_flags, out_flags = gather(far, near, tokens, out_grad, (mask_in, mask_out))
    act, hid = row_stage(chips, cores, gathered, grad_rows, w_in, in_flags, w_out, out_flags)
    mixed, tokens_grad = column_stage(far, near, act, hid, w_out, out_flags, w_in, in_flags)
    w_in_grad, w_out_grad = outers(gathered, hid, in_flags, act, grad_rows, out_flags)
    return (mixed, tokens_grad, w_in_grad, w_out_grad)


def solution(mesh):
    columns, rows = mesh.shape["col"], mesh.shape["row"]
    near = 2 ** (int(math.log2(columns)) // 2)
    return jax.shard_map(
        functools.partial(local, columns // near, near, rows // 2, 2),
        mesh=mesh,
        in_specs=(
            P("col", "row"),
            P("row", "col"),
            P("col", "row"),
            P("row", "col"),
            P("col", "row"),
            P("col", "row"),
        ),
        out_specs=(P("col", "row"), P("col", "row"), P("row", "col"), P("col", "row")),
        check_vma=False,
    )
```

time: 155 us -> 134 us (0.86)
  Pallas kernels: 147 us -> 130 us
  local copies, waits for them, and re-layouts: 5.32 us -> 3.08 us
    pallas_call x4 -> x2, Pallas kernels: 98.8 us -> 80.3 us  [the longest x1 40.9 us: row_stage(): pl.pallas_call(functools.partial(row_kernel, chips, cores, tile, tiles, p...]
    reshape x1 -> x0, local copies, waits for them, and re-layouts: 3.29 us -> none  [spread(): jnp.broadcast_to(flags, (rows, SUB, cols, BLK))]
    unnamed x6 -> x2, local copies, waits for them, and re-layouts: 1.29 us -> 3.08 us
where the time goes in v2:
time: 134 us
  Pallas kernels  130 us (97%)
  local copies, waits for them, and re-layouts  3.08 us (2%)
    pallas_call x1, Pallas kernels, row_stage(): pl.pallas_call(functools.partial(row_kernel, chips, cores, tile, tiles, p...  40.9 us
    pallas_call x1, Pallas kernels, column_stage(): pl.pallas_call(functools.partial(column_kernel, far, near, tile, tiles, p...  39.4 us
    pallas_call x1, Pallas kernels, gather(): pl.pallas_call(functools.partial(gather_kernel, far, near), out_shape=(ou...  31.2 us
    pallas_call x1, Pallas kernels, outers(): pl.pallas_call(outer_kernel, grid=(steps,), out_shape=[jax.ShapeDtypeStru...  18.3 us
    unnamed x2, local copies, waits for them, and re-layouts  3.08 us

profile of v2, /device:TPU:0, one launch (start us, length us, event | category | flops | bytes accessed | tf_op | source)
XLA Modules:
  0.0 133.6 jit_solution(11698577179629319872)
XLA Ops:
  0.6 31.2 %gather_col.1 = (bf16[8,16,3072]{2,1,0:T(8,128)(2,1)}, bf16[8,16,3072]{2,1,0:T(8,128)(2,1)}, bf16[384,3072]{1,0:T(8,128)(2,1)}, bf16[384,3072]{1,0:T(8,128)(2,1)}) custom-call(bf16[16,3072]{1,0:T(8,128)(2,1)} %refs_0_.3, bf16[16,3072]{1,0:T(8,128)(2,1)} %refs_1_.1, s32[24,24]{1,0:T(8,128)} %refs_2_.3, s32[24,24]{1,0:T(8,128)} %refs_3_.1), custom_call_target="tpu_custom_call" | custom-call | tf_op jit(solution)/shard_map/gather_col/pallas_call | solution.py:78
  31.8 40.9 %row_stage.1 = (bf16[4,32,3072]{2,1,0:T(8,128)(2,1)}, bf16[4,32,3072]{2,1,0:T(8,128)(2,1)}) custom-call(bf16[128,3072]{1,0:T(8,128)(2,1)} %bitcast.8, bf16[128,3072]{1,0:T(8,128)(2,1)} %bitcast.10, bf16[3072,3072]{1,0:T(8,128)(2,1)} %refs_2_.5, bf16[384,3072]{1,0:T(8,128)(2,1)} %get-tuple-element.16.refs_1_.refs_3_.in_flags, bf16[3072,3072]{1,0:T(8,128)(2,1)} %refs_0_.5, ...), custom_call_target="tpu_custom_call" | custom-call | tf_op jit(solution)/shard_map/row_stage/pallas_call | solution.py:270
  72.7 18.3 %outers.1 = (bf16[3072,3072]{1,0:T(8,128)(2,1)}, bf16[3072,3072]{1,0:T(8,128)(2,1)}) custom-call(bf16[128,3072]{1,0:T(8,128)(2,1)} %bitcast.9, bf16[128,3072]{1,0:T(8,128)(2,1)} %bitcast.6, bf16[384,3072]{1,0:T(8,128)(2,1)} %get-tuple-element.16.refs_1_.refs_3_.in_flags, bf16[128,3072]{1,0:T(8,128)(2,1)} %bitcast.4, bf16[128,3072]{1,0:T(8,128)(2,1)} %bitcast.11, ...), custom_call_target="tpu_custom_call" | custom-call | tf_op jit(solution)/shard_map/outers/pallas_call | solution.py:406
  91.0 39.4 %column_stage.1 = (bf16[16,3072]{1,0:T(8,128)(2,1)}, bf16[16,3072]{1,0:T(8,128)(2,1)}) custom-call(bf16[128,3072]{1,0:T(8,128)(2,1)} %bitcast.5, bf16[128,3072]{1,0:T(8,128)(2,1)} %bitcast.7, bf16[3072,3072]{1,0:T(8,128)(2,1)} %refs_0_.5, bf16[384,3072]{1,0:T(8,128)(2,1)} %get-tuple-element.17.refs_3_.refs_1_.out_flags, bf16[3072,3072]{1,0:T(8,128)(2,1)} %refs_2_.5, ...), custom_call_target="tpu_custom_call" | custom-call | tf_op jit(solution)/shard_map/column_stage/pallas_call | solution.py:371
  130.5 1.5 %copy.12 = bf16[16,3072]{1,0:T(8,128)(2,1)} copy(bf16[16,3072]{1,0:T(8,128)(2,1)} %get-tuple-element.28) | data formatting | bytes 196608
  132.0 1.5 %copy.13 = bf16[16,3072]{1,0:T(8,128)(2,1)} copy(bf16[16,3072]{1,0:T(8,128)(2,1)} %get-tuple-element.29) | data formatting | bytes 196608

commit v3 on v2

--- a/solution.py
+++ b/solution.py
@@ -28,66 +28,6 @@
     for peer in peers:
         pl.semaphore_signal(barrier, inc=1, device_id={axis: peer}, device_id_type=MESH)
     pl.semaphore_wait(barrier, len(peers))
-
-
-def gather_kernel(far, near, *refs):
-    srcs, masks, dsts, flags, (zs, zr, ys, yr, own) = refs[:2], refs[2:4], refs[4:6], refs[6:8], refs[8:]
-    me = lax.axis_index("col")
-    z, y = me // near, lax.rem(me, near)
-    along_z = [lax.rem(z + d, far) * near + y for d in range(1, far)]
-    along_y = [z * near + lax.rem(y + e, near) for e in range(1, near)]
-    greet("col", along_z + along_y)
-    sent = []
-    for a in range(2):
-        for e, peer in enumerate(along_y):
-            sent.append(remote(srcs[a], dsts[a].at[me], ys.at[a, 0, e], yr.at[a, 0, e], "col", peer))
-            sent[-1].start()
-        for d, peer in enumerate(along_z):
-            sent.append(remote(srcs[a], dsts[a].at[me], zs.at[a, d], zr.at[a, d], "col", peer))
-            sent[-1].start()
-    kept = [pltpu.make_async_copy(srcs[a], dsts[a].at[me], own.at[a]) for a in range(2)]
-    for copy in kept:
-        copy.start()
-    for a in range(2):
-        flags[a][...] = spread(masks[a][...])
-    for a in range(2):
-        for d in range(far - 1):
-            block = lax.rem(z + far - d - 1, far) * near + y
-            slot = dsts[a].at[block]
-            remote(srcs[a], slot, zs.at[a, d], zr.at[a, d], "col", along_z[d]).wait_recv()
-            for e, peer in enumerate(along_y):
-                sent.append(remote(slot, slot, ys.at[a, d + 1, e], yr.at[a, d + 1, e], "col", peer))
-                sent[-1].start()
-    for a in range(2):
-        for d in range(far):
-            for e in range(near - 1):
-                block = lax.rem(z + far - d, far) * near + lax.rem(y + near - e - 1, near)
-                slot = dsts[a].at[block]
-                remote(slot, slot, ys.at[a, d, e], yr.at[a, d, e], "col", along_y[e]).wait_recv()
-    for copy in sent:
-        copy.wait_send()
-    for copy in kept:
-        copy.wait()
-
-
-def gather(far, near, first, second, masks):
-    out = jax.ShapeDtypeStruct((far * near,) + first.shape, first.dtype)
-    spreads = tuple(
-        jax.ShapeDtypeStruct((each.shape[0] * SUB, each.shape[1] * BLK), jnp.bfloat16) for each in masks
-    )
-    *gathered, in_flags, out_flags = pl.pallas_call(
-        functools.partial(gather_kernel, far, near),
-        out_shape=(out, out) + spreads,
-        in_specs=[VMEM] * 4,
-        out_specs=(VMEM,) * 4,
-        scratch_shapes=[
-            DMA((2, far - 1)), DMA((2, far - 1)),
-            DMA((2, far, near - 1)), DMA((2, far, near - 1)), DMA((2,)),
-        ],
-        compiler_params=pltpu.CompilerParams(collective_id=0, has_side_effects=True),
-        name="gather_col",
-    )(first, second, *masks)
-    return [each.reshape(-1, first.shape[1]) for each in gathered] + [in_flags, out_flags]
 
 
 def spread(mask):
@@ -167,27 +107,68 @@
     return value * half, slope
 
 
-def row_kernel(chips, cores, tile, tiles, pieces, left, right, *refs):
-    sources, outs, refs = refs[:4], refs[4:6], refs[6:]
-    buffers, refs = refs[:5], refs[5:]
-    parts, pair, sums, landed, ps, pr, xs, xr, gs, gr, fs, fr = refs
+def front_kernel(far, near, chips, cores, tile, tiles, pieces, *refs):
+    srcs, masks, weights, outs, dsts, flags = (refs[n:n + 2] for n in range(0, 12, 2))
+    down_slots, up_slots, arrived, zs, zr, ys, yr, own = refs[12:20]
+    parts, pair, sums, landed, slopes, ps, pr, xs, xr, gs, gr, fs, fr = refs[20:]
+    slots = (down_slots, up_slots)
+    mine = lax.axis_index("col")
+    z, y = mine // near, lax.rem(mine, near)
+    along_z = [lax.rem(z + d, far) * near + y for d in range(1, far)]
+    along_y = [z * near + lax.rem(y + e, near) for e in range(1, near)]
     me = lax.axis_index("row")
     x, k = me // cores, lax.rem(me, cores)
     partner = x * cores + (1 - k)
     across = [lax.rem(x + d, chips) for d in range(1, chips)]
     peers = [c * cores + k for c in across]
-    first, multiply = streamed(tile, tiles, left, right, sources, buffers)
-    first()
-    greet("row", [partner] + peers)
     per = tiles // pieces
     cols = per * tile
     shaped = parts.shape[2:5]
+    rows = tile // BLK * SUB
     sent = []
 
     def push(copy):
         copy.start()
         sent.append(copy)
 
+    def fetch(a, t):
+        slot = lax.rem(t, 2)
+        spot = pl.ds(pl.multiple_of(t * tile, tile), tile)
+        view = weights[0].at[:, spot] if a == 0 else weights[1].at[spot, :]
+        return pltpu.make_async_copy(view, slots[a].at[slot], arrived.at[a, slot])
+
+    for a in range(2):
+        fetch(a, jnp.int32(0)).start()
+    barrier = pltpu.get_barrier_semaphore()
+    for axis, group in (("col", along_z + along_y), ("row", [partner] + peers)):
+        for peer in group:
+            pl.semaphore_signal(barrier, inc=1, device_id={axis: peer}, device_id_type=MESH)
+    pl.semaphore_wait(barrier, len(along_z) + len(along_y) + len(peers) + 1)
+
+    for a in range(2):
+        for e, peer in enumerate(along_y):
+            push(remote(srcs[a], dsts[a].at[mine], ys.at[a, 0, e], yr.at[a, 0, e], "col", peer))
+        for d, peer in enumerate(along_z):
+            push(remote(srcs[a], dsts[a].at[mine], zs.at[a, d], zr.at[a, d], "col", peer))
+    kept = [pltpu.make_async_copy(srcs[a], dsts[a].at[mine], own.at[a]) for a in range(2)]
+    for copy in kept:
+        copy.start()
+    for a in range(2):
+        flags[a][...] = spread(masks[a][...])
+
+    def relay(a, d):
+        slot = dsts[a].at[lax.rem(z + far - d - 1, far) * near + y]
+        remote(srcs[a], slot, zs.at[a, d], zr.at[a, d], "col", along_z[d]).wait_recv()
+        for e, peer in enumerate(along_y):
+            push(remote(slot, slot, ys.at[a, d + 1, e], yr.at[a, d + 1, e], "col", peer))
+
+    def gathered(a):
+        for d in range(far):
+            for e in range(near - 1):
+                slot = dsts[a].at[lax.rem(z + far - d, far) * near + lax.rem(y + near - e - 1, near)]
+                remote(slot, slot, ys.at[a, d, e], yr.at[a, d, e], "col", along_y[e]).wait_recv()
+        kept[a].wait()
+
     def to_partner(a, p):
         return remote(parts.at[a, p, :, 1 - k], pair.at[a, p], ps.at[a, p], pr.at[a, p], "row", partner)
 
@@ -203,56 +184,75 @@
     def give_partner(a, p, d, owner):
         return remote(share(a, p, owner), share(a, p, owner), fs.at[a, p, d], fr.at[a, p, d], "row", partner)
 
-    def compute(p):
+    def compute(a, p):
+        if p == 0:
+            gathered(a)
+
         def step(j, carry):
-            spot = pl.ds(pl.multiple_of(j * tile, tile), tile)
-            for a, value in enumerate(multiply(p * per + j)):
-                parts[a, p, :, :, :, spot] = value.reshape(*shaped, tile)
+            t = p * per + j
+            slot = lax.rem(t, 2)
+            fetch(a, t).wait()
+
+            @pl.when(t + 1 < tiles)
+            def _():
+                fetch(a, t + 1).start()
+
+            left = dsts[a][...].reshape(-1, dsts[a].shape[-1])
+            if a == 0:
+                marks = flags[0][:, pl.ds(pl.multiple_of(t * tile, tile), tile)]
+            else:
+                marks = flags[1][pl.ds(pl.multiple_of(t * rows, rows), rows), :]
+            value = lax.dot_general(
+                left, masked(slots[a][slot], marks), (((1,), (a,)), ((), ())), preferred_element_type=jnp.float32
+            )
+            parts[a, p, :, :, :, pl.ds(pl.multiple_of(j * tile, tile), tile)] = value.reshape(*shaped, tile)
             return carry
 
         lax.fori_loop(0, per, step, 0)
-        for a in range(2):
-            push(to_partner(a, p))
-
-    def reduce_pair(p):
-        for a in range(2):
-            to_partner(a, p).wait_recv()
-            for d, c in enumerate(across):
-                sums[a, p, d] = (parts[a, p, c, k] + pair[a, p, c]).astype(sums.dtype)
-                push(to_chip(a, p, d))
-
-    def finish(p):
-        totals = []
-        for a in range(2):
-            total = parts[a, p, x, k] + pair[a, p, x]
-            for d in range(chips - 1):
-                to_chip(a, p, d).wait_recv()
-                total = total + landed[a, p, d].astype(jnp.float32)
-            totals.append(total)
-        act, slope = gelu_parts(totals[0])
-        for a, value in enumerate((act, totals[1] * slope)):
-            outs[a][me, :, pl.ds(p * cols, cols)] = value.astype(outs[a].dtype)
-            for d in range(chips - 1):
-                push(give_chip(a, p, d, me))
-            push(give_partner(a, p, chips - 1, me))
-
-    def forward(p):
-        for a in range(2):
-            for d in range(chips - 1):
-                owner = lax.rem(x + chips - d - 1, chips) * cores + k
-                give_chip(a, p, d, owner).wait_recv()
-                push(give_partner(a, p, d, owner))
-
+        push(to_partner(a, p))
+        if a == 0:
+            for d in range(far - 1):
+                if d * pieces // (far - 1) == p:
+                    relay(1, d)
+
+    def reduce_pair(a, p):
+        to_partner(a, p).wait_recv()
+        for d, c in enumerate(across):
+            sums[a, p, d] = (parts[a, p, c, k] + pair[a, p, c]).astype(sums.dtype)
+            push(to_chip(a, p, d))
+
+    def finish(a, p):
+        total = parts[a, p, x, k] + pair[a, p, x]
+        for d in range(chips - 1):
+            to_chip(a, p, d).wait_recv()
+            total = total + landed[a, p, d].astype(jnp.float32)
+        if a == 0:
+            value, slopes[p] = gelu_parts(total)
+        else:
+            value = total * slopes[p]
+        outs[a][me, :, pl.ds(p * cols, cols)] = value.astype(outs[a].dtype)
+        for d in range(chips - 1):
+            push(give_chip(a, p, d, me))
+        push(give_partner(a, p, chips - 1, me))
+
+    def forward(a, p):
+        for d in range(chips - 1):
+            owner = lax.rem(x + chips - d - 1, chips) * cores + k
+            give_chip(a, p, d, owner).wait_recv()
+            push(give_partner(a, p, d, owner))
+
+    for d in range(far - 1):
+        relay(0, d)
     stages = (compute, reduce_pair, finish, forward)
-    for step in range(pieces + len(stages) - 1):
+    jobs = [(a, p) for a in range(2) for p in range(pieces)]
+    for step in range(len(jobs) + len(stages) - 1):
         for lag, stage in enumerate(stages):
-            if 0 <= step - lag < pieces:
-                stage(step - lag)
-    for p in range(pieces):
-        for a in range(2):
-            for d in range(chips):
-                owner = lax.rem(x + chips - lax.rem(d + 1, chips), chips) * cores + (1 - k)
-                give_partner(a, p, d, owner).wait_recv()
+            if 0 <= step - lag < len(jobs):
+                stage(*jobs[step - lag])
+    for a, p in jobs:
+        for d in range(chips):
+            owner = lax.rem(x + chips - lax.rem(d + 1, chips), chips) * cores + (1 - k)
+            give_partner(a, p, d, owner).wait_recv()
     for copy in sent:
         copy.wait_send()
 
@@ -260,32 +260,41 @@
 ANY = pl.BlockSpec(memory_space=pl.ANY)
 
 
-def row_stage(chips, cores, left, right, down, down_flags, up, up_flags):
-    tokens, depth = left.shape
-    width = down.shape[1]
+def front_stage(far, near, chips, cores, first, second, masks, down, up):
+    depth, width = down.shape
+    tokens = first.shape[0] * far * near
     tile, tiles, pieces = tiling(width)
     cols = width // pieces
     share = tokens // (chips * cores)
     out = jax.ShapeDtypeStruct((chips * cores, share, width), jnp.bfloat16)
-    gathered = pl.pallas_call(
-        functools.partial(row_kernel, chips, cores, tile, tiles, pieces),
-        out_shape=(out, out),
-        in_specs=[VMEM] * 2 + [ANY] * 4,
-        out_specs=(VMEM, VMEM),
-        scratch_shapes=stream_shapes(depth, tile) + [
+    full = jax.ShapeDtypeStruct((far * near,) + first.shape, first.dtype)
+    spreads = tuple(
+        jax.ShapeDtypeStruct((each.shape[0] * SUB, each.shape[1] * BLK), jnp.bfloat16) for each in masks
+    )
+    act, hid, gathered, grad_rows, in_flags, out_flags = pl.pallas_call(
+        functools.partial(front_kernel, far, near, chips, cores, tile, tiles, pieces),
+        out_shape=(out, out, full, full) + spreads,
+        in_specs=[VMEM] * 4 + [ANY] * 2,
+        out_specs=(VMEM,) * 6,
+        scratch_shapes=[
+            pltpu.VMEM((2, depth, tile), jnp.bfloat16), pltpu.VMEM((2, tile, depth), jnp.bfloat16), DMA((2, 2)),
+            DMA((2, far - 1)), DMA((2, far - 1)),
+            DMA((2, far, near - 1)), DMA((2, far, near - 1)), DMA((2,)),
             pltpu.VMEM((2, pieces, chips, cores, share, cols), jnp.float32),
             pltpu.VMEM((2, pieces, chips, share, cols), jnp.float32),
             pltpu.VMEM((2, pieces, chips - 1, share, cols), jnp.bfloat16),
             pltpu.VMEM((2, pieces, chips - 1, share, cols), jnp.bfloat16),
+            pltpu.VMEM((pieces, share, cols), jnp.float32),
             DMA((2, pieces)), DMA((2, pieces)),
             DMA((2, pieces, chips - 1)), DMA((2, pieces, chips - 1)),
             DMA((2, pieces, chips - 1)), DMA((2, pieces, chips - 1)),
             DMA((2, pieces, chips)), DMA((2, pieces, chips)),
         ],
-        compiler_params=pltpu.CompilerParams(collective_id=1, has_side_effects=True),
-        name="row_stage",
-    )(left, right, down, down_flags, up, up_flags)
-    return [each.reshape(tokens, width) for each in gathered]
+        compiler_params=pltpu.CompilerParams(collective_id=0, has_side_effects=True),
+        name="front_stage",
+    )(first, second, *masks, down, up)
+    flat = lambda each: each.reshape(tokens, each.shape[-1])
+    return flat(act), flat(hid), flat(gathered), flat(grad_rows), in_flags, out_flags
 
 
 def column_kernel(far, near, tile, tiles, pieces, left, right, *refs):
@@ -425,8 +434,9 @@
 
 
 def local(far, near, chips, cores, tokens, w_in, w_out, mask_in, mask_out, out_grad):
-    gathered, grad_rows, in_flags, out_flags = gather(far, near, tokens, out_grad, (mask_in, mask_out))
-    act, hid = row_stage(chips, cores, gathered, grad_rows, w_in, in_flags, w_out, out_flags)
+    act, hid, gathered, grad_rows, in_flags, out_flags = front_stage(
+        far, near, chips, cores, tokens, out_grad, (mask_in, mask_out), w_in, w_out
+    )
     mixed, tokens_grad = column_stage(far, near, act, hid, w_out, out_flags, w_in, in_flags)
     w_in_grad, w_out_grad = outers(gathered, hid, in_flags, act, grad_rows, out_flags)
     return (mixed, tokens_grad, w_in_grad, w_out_grad)

time: 134 us -> 132 us (0.985)
  Pallas kernels: 130 us -> 127 us
    pallas_call x2 -> x1, Pallas kernels: 72 us -> 69 us  [front_stage(): pl.pallas_call(functools.partial(front_kernel, far, near, chips, cores, t...]
where the time goes in v3:
time: 132 us; the launch traced here: 131 us
  Pallas kernels  127 us (96%)
  local copies, waits for them, and re-layouts  3.08 us (2%)
    pallas_call x1, Pallas kernels, front_stage(): pl.pallas_call(functools.partial(front_kernel, far, near, chips, cores, t...  69 us
    pallas_call x1, Pallas kernels, column_stage(): pl.pallas_call(functools.partial(column_kernel, far, near, tile, tiles, p...  40 us
    pallas_call x1, Pallas kernels, outers(): pl.pallas_call(outer_kernel, grid=(steps,), out_shape=[jax.ShapeDtypeStru...  18.3 us
    unnamed x2, local copies, waits for them, and re-layouts  3.08 us

profile of v3, /device:TPU:0, one launch (start us, length us, event | category | flops | bytes accessed | tf_op | source)
XLA Modules:
  0.0 131.0 jit_solution(16117066487990812011)
XLA Ops:
  0.6 69.0 %front_stage.1 = (bf16[4,32,3072]{2,1,0:T(8,128)(2,1)}, bf16[4,32,3072]{2,1,0:T(8,128)(2,1)}, bf16[8,16,3072]{2,1,0:T(8,128)(2,1)}, bf16[8,16,3072]{2,1,0:T(8,12...) custom-call(bf16[16,3072]{1,0:T(8,128)(2,1)} %refs_0_.2, bf16[16,3072]{1,0:T(8,128)(2,1)} %refs_1_.1, ...), custom_call_target="tpu_custom_call" | custom-call | tf_op jit(solution)/shard_map/front_stage/pallas_call | solution.py:274
  69.6 18.3 %outers.1 = (bf16[3072,3072]{1,0:T(8,128)(2,1)}, bf16[3072,3072]{1,0:T(8,128)(2,1)}) custom-call(bf16[128,3072]{1,0:T(8,128)(2,1)} %bitcast.8, bf16[128,3072]{1,0:T(8,128)(2,1)} %bitcast.6, bf16[384,3072]{1,0:T(8,128)(2,1)} %get-tuple-element.17.refs_3_.in_flags, bf16[128,3072]{1,0:T(8,128)(2,1)} %bitcast.4, bf16[128,3072]{1,0:T(8,128)(2,1)} %bitcast.9, ...), custom_call_target="tpu_custom_call" | custom-call | tf_op jit(solution)/shard_map/outers/pallas_call | solution.py:415
  88.0 40.0 %column_stage.1 = (bf16[16,3072]{1,0:T(8,128)(2,1)}, bf16[16,3072]{1,0:T(8,128)(2,1)}) custom-call(bf16[128,3072]{1,0:T(8,128)(2,1)} %bitcast.5, bf16[128,3072]{1,0:T(8,128)(2,1)} %bitcast.7, bf16[3072,3072]{1,0:T(8,128)(2,1)} %refs_0_.3, bf16[384,3072]{1,0:T(8,128)(2,1)} %get-tuple-element.16.refs_1_.out_flags, bf16[3072,3072]{1,0:T(8,128)(2,1)} %refs_2_.3, ...), custom_call_target="tpu_custom_call" | custom-call | tf_op jit(solution)/shard_map/column_stage/pallas_call | solution.py:380
  128.0 1.5 %copy.12 = bf16[16,3072]{1,0:T(8,128)(2,1)} copy(bf16[16,3072]{1,0:T(8,128)(2,1)} %get-tuple-element.28) | data formatting | bytes 196608
  129.5 1.5 %copy.13 = bf16[16,3072]{1,0:T(8,128)(2,1)} copy(bf16[16,3072]{1,0:T(8,128)(2,1)} %get-tuple-element.29) | data formatting | bytes 196608
